TPU v7x, 32 devices: a whole 2x2x4 slice. The times are simulated.
32 devices in a mesh: groups: 2 (over x), gx: 16 (over z, y, core).
Axes of the slice: x: 2, y: 2, z: 4, core: 2. Of those that a mesh axis runs over, the one named last changes fastest.
Arguments:
- features: bfloat16 [64, 16, 64, 128], P(('groups', 'gx')), parts along dimension 0, may hold values from -6 to 6
- cotangent: bfloat16 [64, 16, 64, 128], P(('groups', 'gx')), parts along dimension 0, may hold values from -6 to 6
- wall_flags: int32 [64, 16, 128], P(('groups', 'gx')), parts along dimension 0, may hold values 0 or 1
- mode_counts: int32 [64], replicated, may hold values from 1 to 16, as said below
- offsets: int32 [6, 3], replicated, may hold values from -2 to 2, as said below
- point_weight: bfloat16 [64, 64], replicated, may hold values from -0.75 to 0.75
- kernel_weight: bfloat16 [6, 64, 64], replicated, may hold values from -0.3125 to 0.3125
- lap_weight: bfloat16 [64, 64], replicated, may hold values from -0.125 to 0.125
- spec_weight: bfloat16 [16, 64, 64], replicated, may hold values from -1 to 1
- bias: float32 [64], replicated, may hold values from -3 to 3
Outputs:
- input_grad: bfloat16 [64, 16, 64, 128], P(('groups', 'gx')), parts along dimension 0
- kernel_grad: float32 [12, 64, 64], P('groups'), parts along dimension 0
There are 2 independent parts, one for each index of `groups`. A program takes and returns all parts, laid end to end along the dimension named above; an argument that names none is the same for every part. Nothing has to cross between parts.
Inputs may be any that keep to these rules, and one draw needn't show every extreme that they name: Column 0 holds x offsets in -1..1 and both -1 and 1 occur; columns 1 and 2 hold y and z offsets in -2..2, and -2 and 2 occur in each of them. `mode_counts`: some channel keeps 16 modes and some channel keeps 1.
All inputs are finite; a program needn't handle non-finite values. No bound on the sum of `wall_flags` on one device may be relied on, other than what follows from the above.
Results may differ from a plain program's by a relative error of at most 0.0066.
Values may be sent and summed in bfloat16 or wider, within the bound.
A program may use at most 256 MiB of HBM per device.

v0:
```python
from functools import partial
import math
import jax
import jax.numpy as jnp
from jax import lax
from jax.sharding import PartitionSpec as P

RAD = 2


def with_halo(cells, sides, width):
    for axis, dim in sides:
        count = lax.axis_size(axis)
        ends = count - 1
        head = lax.slice_in_dim(cells, 0, width, axis=dim)
        tail = lax.slice_in_dim(cells, cells.shape[dim] - width, cells.shape[dim], axis=dim)
        cells = jnp.concatenate(
            [
                lax.ppermute(tail, axis, [(i, (i + 1) % count) for i in range(ends)]),
                cells,
                lax.ppermute(head, axis, [((i + 1) % count, i) for i in range(ends)]),
            ],
            axis=dim,
        )
    return cells


def basis_table(mode_total, length):
    mode_index = jnp.arange(mode_total, dtype=jnp.float32)[:, None]
    cell_index = jnp.arange(length, dtype=jnp.float32)[None, :]
    phase_angle = math.pi / (2.0 * length) * mode_index * (2.0 * cell_index + 1.0)
    amplitude = jnp.where(mode_index == 0.0, math.sqrt(1.0 / length), math.sqrt(2.0 / length))
    return (amplitude * jnp.cos(phase_angle)).astype(jnp.bfloat16)


def pencil_work(pencil, spec_weight, kept_modes, adjoint):
    basis = basis_table(spec_weight.shape[0], pencil.shape[0])
    coefficients = jnp.einsum(
        "kx,xycz->kycz", basis, pencil, preferred_element_type=jnp.float32
    ).astype(jnp.bfloat16)
    if adjoint:
        masked = coefficients * kept_modes[:, None, :, None].astype(jnp.bfloat16)
        mixed_modes = jnp.einsum(
            "koc,kyoz->kycz", spec_weight, masked, preferred_element_type=jnp.float32
        ).astype(jnp.bfloat16)
    else:
        mixed_modes = jnp.einsum(
            "koc,kycz->kyoz", spec_weight, coefficients, preferred_element_type=jnp.float32
        )
        mixed_modes = (mixed_modes * kept_modes[:, None, :, None]).astype(jnp.bfloat16)
    return jnp.einsum(
        "kx,kyoz->xyoz", basis, mixed_modes, preferred_element_type=jnp.float32
    ).astype(jnp.bfloat16)


def spectral(slab, spec_weight, kept_modes, adjoint):
    result = pencil_work(
        lax.all_to_all(slab, "gx", split_axis=1, concat_axis=0, tiled=True),
        spec_weight,
        kept_modes,
        adjoint,
    )
    return lax.all_to_all(result, "gx", split_axis=0, concat_axis=1, tiled=True)


def laplace_ext(extended):
    padded = jnp.pad(extended, ((0, 0), (1, 1), (0, 0), (1, 1))).astype(jnp.float32)
    centre_cells = padded[1:-1, 1:-1, :, 1:-1]
    neighbours = padded[2:, 1:-1, :, 1:-1] + padded[:-2, 1:-1, :, 1:-1]
    neighbours = neighbours + padded[1:-1, 2:, :, 1:-1] + padded[1:-1, :-2, :, 1:-1]
    neighbours = neighbours + padded[1:-1, 1:-1, :, 2:] + padded[1:-1, 1:-1, :, :-2]
    return (neighbours - 6.0 * centre_cells).astype(jnp.bfloat16)


def pad_sides(extended):
    return jnp.pad(extended, ((0, 0), (RAD, RAD), (0, 0), (RAD, RAD)))


def window_of(padded, offset, direction, slab_shape):
    starts = (
        1 + direction * offset[0],
        RAD + direction * offset[1],
        0,
        RAD + direction * offset[2],
    )
    return lax.dynamic_slice(padded, starts, slab_shape)


def gelu_slope(preact, upstream):
    _, pullback = jax.vjp(partial(jax.nn.gelu, approximate=True), preact)
    return pullback(upstream)[0]


def sum_over_gx(terms):
    count = lax.axis_size("gx")
    if terms.size % count:
        return lax.psum(terms, "gx")
    pieces = lax.all_to_all(terms.reshape(count, -1), "gx", split_axis=0, concat_axis=0, tiled=True)
    mine = jnp.sum(pieces, axis=0)
    copies = jnp.broadcast_to(mine[None, :], pieces.shape)
    gathered = lax.all_to_all(copies, "gx", split_axis=0, concat_axis=0, tiled=True)
    return gathered.reshape(terms.shape)


def per_device(
    features,
    cotangent,
    wall_flags,
    mode_counts,
    offsets,
    point_weight,
    kernel_weight,
    lap_weight,
    spec_weight,
    bias,
):
    mode_total = spec_weight.shape[0]
    tile_total = kernel_weight.shape[0]
    kept_modes = (jnp.arange(mode_total, dtype=jnp.int32)[:, None] < mode_counts[None, :]).astype(
        jnp.float32
    )
    fluid_mask = (1 - wall_flags).astype(jnp.float32)[:, :, None, :]
    extended = with_halo(features, (("gx", 0),), 1)
    padded_field = pad_sides(extended)
    local_part = jnp.einsum(
        "oc,xycz->xyoz", point_weight, features, preferred_element_type=jnp.float32
    )
    local_part = local_part + jnp.einsum(
        "oc,xycz->xyoz", lap_weight, laplace_ext(extended), preferred_element_type=jnp.float32
    )
    for tile in range(tile_total):
        moved = window_of(padded_field, offsets[tile], 1, features.shape)
        local_part = local_part + jnp.einsum(
            "oc,xycz->xyoz", kernel_weight[tile], moved, preferred_element_type=jnp.float32
        )
    local_part = local_part + bias[:, None]
    spectral_part = spectral(features, spec_weight, kept_modes, False)
    preact = local_part + spectral_part.astype(jnp.float32)
    weighted = (gelu_slope(preact, cotangent.astype(jnp.float32)) * fluid_mask).astype(jnp.bfloat16)
    spec_grad = spectral(weighted, spec_weight, kept_modes, True)
    ext_grad = with_halo(weighted, (("gx", 0),), 1)
    padded_grad = pad_sides(ext_grad)
    input_grad = jnp.einsum(
        "oc,xyoz->xycz", point_weight, weighted, preferred_element_type=jnp.float32
    )
    input_grad = input_grad + jnp.einsum(
        "oc,xyoz->xycz", lap_weight, laplace_ext(ext_grad), preferred_element_type=jnp.float32
    )
    input_grad = input_grad + spec_grad.astype(jnp.float32)
    tile_grads = []
    for tile in range(tile_total):
        back_moved = window_of(padded_grad, offsets[tile], -1, weighted.shape)
        input_grad = input_grad + jnp.einsum(
            "oc,xyoz->xycz", kernel_weight[tile], back_moved, preferred_element_type=jnp.float32
        )
        tile_grads.append(
            jnp.einsum("xyoz,xycz->oc", back_moved, features, preferred_element_type=jnp.float32)
        )
    local_grad = jnp.stack(tile_grads, axis=0)
    scaling = float(
        lax.axis_size("gx") * features.shape[0] * features.shape[1] * features.shape[3]
    ) ** (-0.5)
    summed = sum_over_gx(local_grad)
    return (input_grad.astype(jnp.bfloat16), summed * scaling)


def solution(mesh):
    return jax.shard_map(
        per_device,
        mesh=mesh,
        in_specs=(
            P(("groups", "gx"), None, None, None),
            P(("groups", "gx"), None, None, None),
            P(("groups", "gx"), None, None),
            P(),
            P(),
            P(),
            P(),
            P(),
            P(),
            P(),
        ),
        out_specs=(P(("groups", "gx"), None, None, None), P("groups", None, None)),
        check_vma=False,
    )
```

profile of v0, /device:TPU:0, one launch (start us, length us, event | category | flops | bytes accessed | tf_op | source)
XLA Modules:
  0.0 166.4 jit_solution(13771764491910680602)
XLA Ops:
  0.7 1.1 fusion.148
  1.8 2.4 %collective-permute-start = (bf16[1,16,64,128]{3,2,1,0:T(8,128)(2,1)S(1)}, bf16[1,16,64,128]{3,2,1,0:T(8,128)(2,1)S(1)}, u32[]{:S(2)}, u32[]{:S(2)}) collective-permute-start(bf16[1,16,64,128]{3,2,1,0:T(8,128)(2,1)S(1)} %get-tuple-element.5), channel_id=1, source_target_pairs={{0,1},{1,2},{2,3},{3,4},{4,5},{5,6},{6,7},{7,8},{8,9},{9,10},{10,1... | collective-permute-start | bytes 786440 | tf_op jit(solution)/shard_map/ppermute | solution.py:19
  4.2 1.3 collective-permute-start.1
  5.5 1.9 %copy.40 = bf16[2,16,64,128]{3,2,0,1:T(8,128)(2,1)} copy(bf16[2,16,64,128]{3,2,1,0:T(8,128)(2,1)} %param.10) | data formatting | bytes 1048576 | tf_op args[0]
  7.4 9.4 %all-to-all-start = ((bf16[2,16,64,128]{3,2,0,1:T(8,128)(2,1)}), bf16[2,16,64,128]{3,2,0,1:T(8,128)(2,1)S(1)}, u32[]{:S(2)}, u32[]{:S(2)}) async-start(bf16[2,16,64,128]{3,2,0,1:T(8,128)(2,1)} %copy.40), calls=%async_computation | async-start | bytes 1048576 | tf_op jit(solution)/shard_map/all_to_all | solution.py:58
  16.9 1.3 fusion.76
  42.9 1.5 fusion.48
  44.4 1.4 fusion.49
  49.3 6.0 %all-to-all-start.1 = ((bf16[32,1,64,128]{3,2,1,0:T(8,128)(2,1)}), bf16[32,1,64,128]{3,2,1,0:T(8,128)(2,1)S(1)}, u32[]{:S(2)}, u32[]{:S(2)}) async-start(bf16[32,1,64,128]{3,2,1,0:T(8,128)(2,1)} %copy.44), calls=%async_computation.1 | async-start | bytes 1048576 | tf_op jit(solution)/shard_map/all_to_all | solution.py:63
  56.1 1.4 fusion.50
  57.5 1.4 fusion.51
  58.9 2.8 %convolution_add_fusion.1 = f32[2,16,128,64]{2,3,1,0:T(8,128)} fusion(f32[2,16,128,64]{2,3,1,0:T(8,128)S(1)} %copy-done.4, f32[4,18,64,130]{3,2,1,0:T(8,128)S(1)} %pad_convert_fusion.1, bf16[64,64]{1,0:T(8,128)(2,1)S(1)} %copy-done.15), kind=kOutput, calls=%fused_computation.37 | convolution fusion | flops 35913728 | bytes 9453568 | tf_op jit(solution)/shard_map/oc,xycz->xyoz/dot_general | solution.py:128
  61.8 8.0 %all-to-all-done.1 = bf16[32,1,64,128]{3,2,1,0:T(8,128)(2,1)S(1)} async-done(((bf16[32,1,64,128]{3,2,1,0:T(8,128)(2,1)}), bf16[32,1,64,128]{3,2,1,0:T(8,128)(2,1)S(1)}, u32[]{:S(2)}, u32[]{:S(2)}) %all-to-all-start.1) | async-done | bytes 524320 | tf_op jit(solution)/shard_map/all_to_all | solution.py:63
  70.5 4.2 %fusion.33 = bf16[2,16,64,128]{3,2,1,0:T(8,128)(2,1)S(1)} fusion(bf16[2,16,64,128]{3,2,1,0:T(8,128)(2,1)} %param.11, f32[2,16,128,64]{2,3,1,0:T(8,128)} %fusion.51, f32[2,16,128,64]{2,3,1,0:T(8,128)} %fusion.50, f32[2,16,128,64]{2,3,1,0:T(8,128)} %fusion.49, f32[2,16,128,64]{2,3,1,0:T(8,128)} %fusion.48, f32[2,16,128,64]{2,3,1,0:T(8,128)S(1)} %fusion.47, ...), kind=kOutput, calls=%fused_computation.72 | convolution fusion | flops 41680896 | bytes 8946188 | tf_op jit(solution)/shard_map/oc,xycz->xyoz/dot_general | solution.py:133
  74.8 1.9 %collective-permute-start.2 = (bf16[1,16,64,128]{3,2,1,0:T(8,128)(2,1)S(1)}, bf16[1,16,64,128]{3,2,1,0:T(8,128)(2,1)S(1)}, u32[]{:S(2)}, u32[]{:S(2)}) collective-permute-start(bf16[1,16,64,128]{3,2,1,0:T(8,128)(2,1)S(1)} %get-tuple-element.2), channel_id=1, source_target_pairs={{0,1},{1,2},{2,3},{3,4},{4,5},{5,6},{6,7},{7,8},{8,9},{9,10},{10,1... | collective-permute-start | bytes 786440 | tf_op jit(solution)/shard_map/ppermute | solution.py:19
  76.7 1.3 collective-permute-start.3
  92.6 6.9 %all-to-all-start.4 = ((f32[16,1,1536]{2,1,0:T(1,128)}), f32[16,1,1536]{2,1,0:T(1,128)S(1)}, u32[]{:S(2)}, u32[]{:S(2)}) async-start(f32[16,1,1536]{2,1,0:T(1,128)} %all_to_all.57), calls=%async_computation.4 | async-start | bytes 196608 | tf_op jit(solution)/shard_map/all_to_all | solution.py:98
  100.3 6.6 %all-to-all-done.4 = f32[16,1,1536]{2,1,0:T(1,128)S(1)} async-done(((f32[16,1,1536]{2,1,0:T(1,128)}), f32[16,1,1536]{2,1,0:T(1,128)S(1)}, u32[]{:S(2)}, u32[]{:S(2)}) %all-to-all-start.4) | async-done | bytes 98336 | tf_op jit(solution)/shard_map/all_to_all | solution.py:98
  107.6 3.8 %all-to-all-start.2 = ((bf16[2,16,64,128]{3,2,0,1:T(8,128)(2,1)}), bf16[2,16,64,128]{3,2,0,1:T(8,128)(2,1)S(1)}, u32[]{:S(2)}, u32[]{:S(2)}) async-start(bf16[2,16,64,128]{3,2,0,1:T(8,128)(2,1)} %copy.49), calls=%async_computation.2 | async-start | bytes 1048576 | tf_op jit(solution)/shard_map/all_to_all | solution.py:58
  111.4 1.3 fusion.74
  113.2 1.4 convolution_bitcast_fusion.2
  114.7 10.8 %all-to-all-done.2 = bf16[2,16,64,128]{3,2,0,1:T(8,128)(2,1)S(1)} async-done(((bf16[2,16,64,128]{3,2,0,1:T(8,128)(2,1)}), bf16[2,16,64,128]{3,2,0,1:T(8,128)(2,1)S(1)}, u32[]{:S(2)}, u32[]{:S(2)}) %all-to-all-start.2) | async-done | bytes 524320 | tf_op jit(solution)/shard_map/all_to_all | solution.py:58
  126.3 4.0 %all-to-all-start.5 = ((f32[16,1,1536]{2,1,0:T(1,128)}), f32[16,1,1536]{2,1,0:T(1,128)S(1)}, u32[]{:S(2)}, u32[]{:S(2)}) async-start(f32[16,1,1536]{2,1,0:T(1,128)} %broadcast_in_dim.14), calls=%async_computation.5 | async-start | bytes 196608 | tf_op jit(solution)/shard_map/all_to_all | solution.py:101
  132.5 5.2 %all-to-all-done.5 = f32[16,1,1536]{2,1,0:T(1,128)S(1)} async-done(((f32[16,1,1536]{2,1,0:T(1,128)}), f32[16,1,1536]{2,1,0:T(1,128)S(1)}, u32[]{:S(2)}, u32[]{:S(2)}) %all-to-all-start.5) | async-done | bytes 98336 | tf_op jit(solution)/shard_map/all_to_all | solution.py:101
  137.7 3.6 %all-to-all-start.3 = ((bf16[32,1,64,128]{3,2,1,0:T(8,128)(2,1)}), bf16[32,1,64,128]{3,2,1,0:T(8,128)(2,1)S(1)}, u32[]{:S(2)}, u32[]{:S(2)}) async-start(bf16[32,1,64,128]{3,2,1,0:T(8,128)(2,1)} %copy.55), calls=%async_computation.3 | async-start | bytes 1048576 | tf_op jit(solution)/shard_map/all_to_all | solution.py:63
  141.3 2.9 %pad_convert_fusion = f32[4,18,64,130]{3,2,1,0:T(8,128)} fusion(bf16[4,16,64,128]{3,2,1,0:T(8,128)(2,1)S(1)} %pad_maximum_fusion), kind=kLoop, calls=%fused_computation.12 | loop fusion | flops 599040 | bytes 3444736 | tf_op jit(solution)/shard_map/convert_element_type | solution.py:67
  144.2 1.4 convolution_bitcast_fusion.3
  145.6 1.5 convolution_bitcast_fusion.4
  147.1 1.4 convolution_bitcast_fusion
  149.5 6.2 %all-to-all-done.3 = bf16[32,1,64,128]{3,2,1,0:T(8,128)(2,1)S(1)} async-done(((bf16[32,1,64,128]{3,2,1,0:T(8,128)(2,1)}), bf16[32,1,64,128]{3,2,1,0:T(8,128)(2,1)S(1)}, u32[]{:S(2)}, u32[]{:S(2)}) %all-to-all-start.3) | async-done | bytes 524320 | tf_op jit(solution)/shard_map/all_to_all | solution.py:63
  155.7 7.5 %fusion.15 = f32[2,16,64,128]{3,2,1,0:T(8,128)S(1)} fusion(f32[2,16,128,64]{2,3,1,0:T(8,128)} %fusion.74, f32[4,18,64,130]{3,2,1,0:T(8,128)} %pad_convert_fusion, bf16[64,64]{1,0:T(8,128)(2,1)S(1)} %copy-done.16, bf16[16,2,1,64,128]{4,3,1,0,2:T(8,128)(2,1)S(1)} %bitcast.307), kind=kOutput, calls=%fused_computation.40 | convolution fusion | flops 36438016 | bytes 9969664 | tf_op jit(solution)/shard_map/oc,xyoz->xycz/dot_general | solution.py:146
  163.2 3.2 %fusion.16 = bf16[2,16,64,128]{3,2,1,0:T(8,128)(2,1)} fusion(f32[2,16,64,128]{3,2,1,0:T(8,128)S(1)} %copy-done.2, f32[2,16,64,128]{3,2,1,0:T(8,128)S(1)} %convolution_bitcast_fusion.1, f32[2,16,64,128]{3,2,1,0:T(8,128)} %convolution_bitcast_fusion.2, f32[2,16,64,128]{3,2,1,0:T(8,128)} %convolution_bitcast_fusion.3, ...), kind=kOutput, calls=%fused_computation.43 | convolution fusion | flops 35389440 | bytes 7880716 | tf_op jit(solution)/shard_map/oc,xyoz->xycz/dot_general | solution.py:153
  (73 shorter events, 16.8 us)
Async XLA Ops:
  0.6 46.3 %copy-start = (bf16[16,64,64]{2,1,0:T(8,128)(2,1)S(1)}, bf16[16,64,64]{2,1,0:T(8,128)(2,1)}, u32[]{:S(2)}) copy-start(bf16[16,64,64]{2,1,0:T(8,128)(2,1)} %param.18) | copy-start | bytes 393220
  0.6 16.2 %copy-start.1 = (bf16[2,16,64,128]{3,2,1,0:T(8,128)(2,1)S(1)}, bf16[2,16,64,128]{3,2,1,0:T(8,128)(2,1)}, u32[]{:S(2)}) copy-start(bf16[2,16,64,128]{3,2,1,0:T(8,128)(2,1)} %param.10) | copy-start | bytes 1572868
  0.7 16.2 %copy-start.14 = (s32[64]{0:T(128)S(1)}, s32[64]{0:T(128)}, u32[]{:S(2)}) copy-start(s32[64]{0:T(128)} %param.13) | copy-start | bytes 772
  0.7 16.2 %copy-start.8 = (bf16[64,64]{1,0:T(8,128)(2,1)S(1)}, bf16[64,64]{1,0:T(8,128)(2,1)}, u32[]{:S(2)}) copy-start(bf16[64,64]{1,0:T(8,128)(2,1)} %param.15) | copy-start | bytes 24580
  0.7 17.4 %copy-start.10 = (s32[2,16,128]{2,1,0:T(8,128)S(1)}, s32[2,16,128]{2,1,0:T(8,128)}, u32[]{:S(2)}) copy-start(s32[2,16,128]{2,1,0:T(8,128)} %param.12) | copy-start | bytes 49156
  0.7 18.0 %copy-start.9 = (s32[6,3]{0,1:T(4,128)S(1)}, s32[6,3]{0,1:T(4,128)}, u32[]{:S(2)}) copy-start(s32[6,3]{0,1:T(4,128)} %param.14) | copy-start | bytes 220
  1.8 40.5 %collective-permute-start = (bf16[1,16,64,128]{3,2,1,0:T(8,128)(2,1)S(1)}, bf16[1,16,64,128]{3,2,1,0:T(8,128)(2,1)S(1)}, u32[]{:S(2)}, u32[]{:S(2)}) collective-permute-start(bf16[1,16,64,128]{3,2,1,0:T(8,128)(2,1)S(1)} %get-tuple-element.5), channel_id=1, source_target_pairs={{0,1},{1,2},{2,3},{3,4},{4,5},{5,6},{6,7},{7,8},{8,9},{9,10},{10,1... | collective-permute-start | bytes 786440 | tf_op jit(solution)/shard_map/ppermute | solution.py:19
  4.2 38.2 %collective-permute-start.1 = (bf16[1,16,64,128]{3,2,1,0:T(8,128)(2,1)S(1)}, bf16[1,16,64,128]{3,2,1,0:T(8,128)(2,1)S(1)}, u32[]{:S(2)}, u32[]{:S(2)}) collective-permute-start(bf16[1,16,64,128]{3,2,1,0:T(8,128)(2,1)S(1)} %get-tuple-element.4), channel_id=1, source_target_pairs={{1,0},{2,1},{3,2},{4,3},{5,4},{6,5},{7,6},{8,7},{9,8},{10,9},{11,1... | collective-permute-start | bytes 786440 | tf_op jit(solution)/shard_map/ppermute | solution.py:21
  7.4 35.1 %copy-start.5 = (bf16[6,64,64]{2,1,0:T(8,128)(2,1)S(1)}, bf16[6,64,64]{2,1,0:T(8,128)(2,1)}, u32[]{:S(2)}) copy-start(bf16[6,64,64]{2,1,0:T(8,128)(2,1)} %param.16) | copy-start | bytes 147460
  7.4 38.4 %all-to-all-start = ((bf16[2,16,64,128]{3,2,0,1:T(8,128)(2,1)}), bf16[2,16,64,128]{3,2,0,1:T(8,128)(2,1)S(1)}, u32[]{:S(2)}, u32[]{:S(2)}) async-start(bf16[2,16,64,128]{3,2,0,1:T(8,128)(2,1)} %copy.40), calls=%async_computation | async-start | bytes 1048576 | tf_op jit(solution)/shard_map/all_to_all | solution.py:58
  49.3 20.5 %all-to-all-start.1 = ((bf16[32,1,64,128]{3,2,1,0:T(8,128)(2,1)}), bf16[32,1,64,128]{3,2,1,0:T(8,128)(2,1)S(1)}, u32[]{:S(2)}, u32[]{:S(2)}) async-start(bf16[32,1,64,128]{3,2,1,0:T(8,128)(2,1)} %copy.44), calls=%async_computation.1 | async-start | bytes 1048576 | tf_op jit(solution)/shard_map/all_to_all | solution.py:63
  56.0 2.9 %copy-start.4 = (f32[2,16,128,64]{2,3,1,0:T(8,128)S(1)}, f32[2,16,128,64]{2,3,1,0:T(8,128)}, u32[]{:S(2)}) copy-start(f32[2,16,128,64]{2,3,1,0:T(8,128)} %fusion.76) | copy-start | bytes 3145732
  56.1 2.9 %copy-start.15 = (bf16[64,64]{1,0:T(8,128)(2,1)S(1)}, bf16[64,64]{1,0:T(8,128)(2,1)}, u32[]{:S(2)}) copy-start(bf16[64,64]{1,0:T(8,128)(2,1)} %param.17) | copy-start | bytes 24580
  57.5 13.0 %copy-start.13 = (f32[64]{0:T(128)S(1)}, f32[64]{0:T(128)}, u32[]{:S(2)}) copy-start(f32[64]{0:T(128)} %param.19) | copy-start | bytes 772
  69.7 0.8 copy-start.3
  74.8 14.5 %collective-permute-start.2 = (bf16[1,16,64,128]{3,2,1,0:T(8,128)(2,1)S(1)}, bf16[1,16,64,128]{3,2,1,0:T(8,128)(2,1)S(1)}, u32[]{:S(2)}, u32[]{:S(2)}) collective-permute-start(bf16[1,16,64,128]{3,2,1,0:T(8,128)(2,1)S(1)} %get-tuple-element.2), channel_id=1, source_target_pairs={{0,1},{1,2},{2,3},{3,4},{4,5},{5,6},{6,7},{7,8},{8,9},{9,10},{10,1... | collective-permute-start | bytes 786440 | tf_op jit(solution)/shard_map/ppermute | solution.py:19
  76.7 12.6 %collective-permute-start.3 = (bf16[1,16,64,128]{3,2,1,0:T(8,128)(2,1)S(1)}, bf16[1,16,64,128]{3,2,1,0:T(8,128)(2,1)S(1)}, u32[]{:S(2)}, u32[]{:S(2)}) collective-permute-start(bf16[1,16,64,128]{3,2,1,0:T(8,128)(2,1)S(1)} %get-tuple-element.3), channel_id=1, source_target_pairs={{1,0},{2,1},{3,2},{4,3},{5,4},{6,5},{7,6},{8,7},{9,8},{10,9},{11,1... | collective-permute-start | bytes 786440 | tf_op jit(solution)/shard_map/ppermute | solution.py:21
  92.6 14.3 %all-to-all-start.4 = ((f32[16,1,1536]{2,1,0:T(1,128)}), f32[16,1,1536]{2,1,0:T(1,128)S(1)}, u32[]{:S(2)}, u32[]{:S(2)}) async-start(f32[16,1,1536]{2,1,0:T(1,128)} %all_to_all.57), calls=%async_computation.4 | async-start | bytes 196608 | tf_op jit(solution)/shard_map/all_to_all | solution.py:98
  106.9 0.6 copy-start.6
  107.6 18.0 %all-to-all-start.2 = ((bf16[2,16,64,128]{3,2,0,1:T(8,128)(2,1)}), bf16[2,16,64,128]{3,2,0,1:T(8,128)(2,1)S(1)}, u32[]{:S(2)}, u32[]{:S(2)}) async-start(bf16[2,16,64,128]{3,2,0,1:T(8,128)(2,1)} %copy.49), calls=%async_computation.2 | async-start | bytes 1048576 | tf_op jit(solution)/shard_map/all_to_all | solution.py:58
  112.8 1.9 %copy-start.7 = (f32[16,1,1536]{2,1,0:T(1,128)S(1)}, f32[16,1,1536]{2,1,0:T(1,128)}, u32[]{:S(2)}) copy-start(f32[16,1,1536]{2,1,0:T(1,128)} %copy-done.6) | copy-start | bytes 294916
  112.8 17.5 %copy-start.11 = (f32[16]{0:T(128)S(1)}, f32[16]{0:T(128)}, u32[]{:S(2)}) copy-start(f32[16]{0:T(128)} %get-tuple-element.27) | copy-start | bytes 196
  112.8 17.5 %copy-start.12 = (f32[32]{0:T(128)S(1)}, f32[32]{0:T(128)}, u32[]{:S(2)}) copy-start(f32[32]{0:T(128)} %multiply_add_fusion) | copy-start | bytes 388
  126.3 11.4 %all-to-all-start.5 = ((f32[16,1,1536]{2,1,0:T(1,128)}), f32[16,1,1536]{2,1,0:T(1,128)S(1)}, u32[]{:S(2)}, u32[]{:S(2)}) async-start(f32[16,1,1536]{2,1,0:T(1,128)} %broadcast_in_dim.14), calls=%async_computation.5 | async-start | bytes 196608 | tf_op jit(solution)/shard_map/all_to_all | solution.py:101
  137.7 18.0 %all-to-all-start.3 = ((bf16[32,1,64,128]{3,2,1,0:T(8,128)(2,1)}), bf16[32,1,64,128]{3,2,1,0:T(8,128)(2,1)S(1)}, u32[]{:S(2)}, u32[]{:S(2)}) async-start(bf16[32,1,64,128]{3,2,1,0:T(8,128)(2,1)} %copy.55), calls=%async_computation.3 | async-start | bytes 1048576 | tf_op jit(solution)/shard_map/all_to_all | solution.py:63
  145.6 10.1 %copy-start.16 = (bf16[64,64]{1,0:T(8,128)(2,1)S(1)}, bf16[64,64]{1,0:T(8,128)(2,1)}, u32[]{:S(2)}) copy-start(bf16[64,64]{1,0:T(8,128)(2,1)} %param.17) | copy-start | bytes 24580
  155.7 7.5 %copy-start.2 = (f32[2,16,64,128]{3,2,1,0:T(8,128)S(1)}, f32[2,16,64,128]{3,2,1,0:T(8,128)}, u32[]{:S(2)}) copy-start(f32[2,16,64,128]{3,2,1,0:T(8,128)} %convolution_bitcast_fusion) | copy-start | bytes 3145732
where the time goes:
time: 168 us; the launch traced here: 166 us
  starting transfers between devices  40.5 us (24%)
  matrix products  38.7 us (23%)
  waiting for transfers between devices  36.7 us (22%)
  between operations  34.7 us (21%)
  local copies, waits for them, and re-layouts  10.6 us (6%)
  other arithmetic  5.23 us (3%)
    all_to_all x2, waiting for transfers between devices, spectral(): return lax.all_to_all(result, 'gx', split_axis=0, concat_axis=1, tiled=True)  14.1 us
    all_to_all x2, starting transfers between devices, spectral(): lax.all_to_all(slab, 'gx', split_axis=1, concat_axis=0, tiled=True)  13.2 us
    all_to_all x2, waiting for transfers between devices, spectral(): lax.all_to_all(slab, 'gx', split_axis=1, concat_axis=0, tiled=True)  10.8 us
    dot_general x6, matrix products, per_device(): jnp.einsum('oc,xycz->xyoz', kernel_weight[tile], moved, preferred_element...  10.4 us
    all_to_all x2, starting transfers between devices, spectral(): return lax.all_to_all(result, 'gx', split_axis=0, concat_axis=1, tiled=True)  9.56 us
    dot_general x6, matrix products, per_device(): jnp.einsum('oc,xyoz->xycz', kernel_weight[tile], back_moved, preferred_el...  9.38 us
    dot_general x1, matrix products, per_device(): jnp.einsum('oc,xyoz->xycz', lap_weight, laplace_ext(ext_grad), preferred_...  7.47 us
    all_to_all x1, starting transfers between devices, sum_over_gx(): lax.all_to_all(terms.reshape(count, -1), 'gx', split_axis=0, concat_axis=...  6.87 us
  transfers between devices with their start and end apart: 10, of which 5 were waited for; matrix products, arithmetic and copies ran while one was open for 18% of the time, Pallas kernels for 0%

commit v1 on v0

--- a/solution.py
+++ b/solution.py
@@ -55,7 +55,10 @@
 
 def spectral(slab, spec_weight, kept_modes, adjoint):
     result = pencil_work(
-        lax.all_to_all(slab, "gx", split_axis=1, concat_axis=0, tiled=True),
+        jnp.concatenate(
+            lax.all_to_all(jnp.stack(jnp.split(slab, lax.axis_size("gx"), axis=1)), "gx", 0, 0),
+            axis=0,
+        ),
         spec_weight,
         kept_modes,
         adjoint,

time: 168 us -> 198 us (1.18)
  local copies, waits for them, and re-layouts: 10.6 us -> 39.6 us
    unnamed x37 -> x62, local copies, waits for them, and re-layouts: 3.47 us -> 30.8 us
    another operation x0 -> x2, local copies, waits for them, and re-layouts: none -> 2 us  [spectral(): jnp.stack(jnp.split(slab, lax.axis_size('gx'), axis=1))]
  transfers between devices with their start and end apart: 10 -> 10, of which waited for: 5 -> 5; matrix products, arithmetic and copies ran while one was open for 18% -> 30% of each run, Pallas kernels for 0% -> 0%
where the time goes in v1:
time: 198 us; the launch traced here: 196 us
  starting transfers between devices  40.3 us (20%)
  local copies, waits for them, and re-layouts  39.6 us (20%)
  matrix products  38.6 us (19%)
  waiting for transfers between devices  37.1 us (19%)
  between operations  35.1 us (18%)
  other arithmetic  5.24 us (3%)
    unnamed x62, local copies, waits for them, and re-layouts  30.8 us
    all_to_all x2, waiting for transfers between devices, spectral(): return lax.all_to_all(result, 'gx', split_axis=0, concat_axis=1, tiled=True)  14.1 us
    all_to_all x2, starting transfers between devices, spectral(): lax.all_to_all(jnp.stack(jnp.split(slab, lax.axis_size('gx'), axis=1)), '...  13 us
    all_to_all x2, waiting for transfers between devices, spectral(): lax.all_to_all(jnp.stack(jnp.split(slab, lax.axis_size('gx'), axis=1)), '...  11.1 us
    dot_general x6, matrix products, per_device(): jnp.einsum('oc,xycz->xyoz', kernel_weight[tile], moved, preferred_element...  10.3 us
    all_to_all x2, starting transfers between devices, spectral(): return lax.all_to_all(result, 'gx', split_axis=0, concat_axis=1, tiled=True)  9.58 us
    dot_general x6, matrix products, per_device(): jnp.einsum('oc,xyoz->xycz', kernel_weight[tile], back_moved, preferred_el...  9.37 us
    dot_general x1, matrix products, per_device(): jnp.einsum('oc,xyoz->xycz', lap_weight, laplace_ext(ext_grad), preferred_...  7.5 us
  transfers between devices with their start and end apart: 10, of which 5 were waited for; matrix products, arithmetic and copies ran while one was open for 30% of the time, Pallas kernels for 0%

profile of v1, /device:TPU:0, one launch (start us, length us, event | category | flops | bytes accessed | tf_op | source)
XLA Modules:
  0.0 196.0 jit_solution(9809728871089283721)
XLA Ops:
  1.8 2.4 %collective-permute-start = (bf16[1,16,64,128]{3,2,1,0:T(8,128)(2,1)S(1)}, bf16[1,16,64,128]{3,2,1,0:T(8,128)(2,1)S(1)}, u32[]{:S(2)}, u32[]{:S(2)}) collective-permute-start(bf16[1,16,64,128]{3,2,1,0:T(8,128)(2,1)S(1)} %get-tuple-element.5), channel_id=1, source_target_pairs={{0,1},{1,2},{2,3},{3,4},{4,5},{5,6},{6,7},{7,8},{8,9},{9,10},{10,1... | collective-permute-start | bytes 786440 | tf_op jit(solution)/shard_map/ppermute | solution.py:19
  5.5 1.4 constant_dynamic-update-slice_fusion.18
  9.6 1.4 constant_dynamic-update-slice_fusion.15
  11.0 1.4 constant_dynamic-update-slice_fusion.14
  12.4 1.4 constant_dynamic-update-slice_fusion.13
  17.9 1.4 constant_dynamic-update-slice_fusion.9
  19.3 1.4 constant_dynamic-update-slice_fusion.8
  27.5 9.4 %all-to-all-start = ((bf16[16,2,1,64,128]{4,3,1,2,0:T(8,128)(2,1)}), bf16[16,2,1,64,128]{4,3,1,2,0:T(8,128)(2,1)S(1)}, u32[]{:S(2)}, u32[]{:S(2)}) async-start(bf16[16,2,1,64,128]{4,3,1,2,0:T(8,128)(2,1)} %constant_dynamic-update-slice_fusion.3), calls=%async_computation | async-start | bytes 1048576 | tf_op jit(solution)/shard_map/all_to_all | solution.py:59
  74.7 1.5 fusion.48
  76.1 1.4 fusion.49
  81.5 6.0 %all-to-all-start.1 = ((bf16[32,1,64,128]{3,2,1,0:T(8,128)(2,1)}), bf16[32,1,64,128]{3,2,1,0:T(8,128)(2,1)S(1)}, u32[]{:S(2)}, u32[]{:S(2)}) async-start(bf16[32,1,64,128]{3,2,1,0:T(8,128)(2,1)} %copy.116), calls=%async_computation.1 | async-start | bytes 1048576 | tf_op jit(solution)/shard_map/all_to_all | solution.py:66
  88.3 1.4 fusion.50
  89.7 1.4 fusion.51
  91.2 2.9 %convolution_add_fusion.1 = f32[2,16,128,64]{2,3,1,0:T(8,128)} fusion(f32[2,16,128,64]{2,3,1,0:T(8,128)S(1)} %copy-done.4, f32[4,18,64,130]{3,2,1,0:T(8,128)S(1)} %pad_convert_fusion.1, bf16[64,64]{1,0:T(8,128)(2,1)S(1)} %copy-done.13), kind=kOutput, calls=%fused_computation.37 | convolution fusion | flops 35913728 | bytes 9453568 | tf_op jit(solution)/shard_map/oc,xycz->xyoz/dot_general | solution.py:131
  94.0 8.0 %all-to-all-done.1 = bf16[32,1,64,128]{3,2,1,0:T(8,128)(2,1)S(1)} async-done(((bf16[32,1,64,128]{3,2,1,0:T(8,128)(2,1)}), bf16[32,1,64,128]{3,2,1,0:T(8,128)(2,1)S(1)}, u32[]{:S(2)}, u32[]{:S(2)}) %all-to-all-start.1) | async-done | bytes 524320 | tf_op jit(solution)/shard_map/all_to_all | solution.py:66
  102.8 4.2 %fusion.33 = bf16[2,16,64,128]{3,2,1,0:T(8,128)(2,1)S(1)} fusion(bf16[2,16,64,128]{3,2,1,0:T(8,128)(2,1)} %param.11, f32[2,16,128,64]{2,3,1,0:T(8,128)} %fusion.51, f32[2,16,128,64]{2,3,1,0:T(8,128)} %fusion.50, f32[2,16,128,64]{2,3,1,0:T(8,128)} %fusion.49, f32[2,16,128,64]{2,3,1,0:T(8,128)} %fusion.48, f32[2,16,128,64]{2,3,1,0:T(8,128)S(1)} %fusion.47, ...), kind=kOutput, calls=%fused_computation.72 | convolution fusion | flops 41680896 | bytes 8946188 | tf_op jit(solution)/shard_map/oc,xycz->xyoz/dot_general | solution.py:136
  107.6 1.9 collective-permute-start.2
  122.8 6.9 %all-to-all-start.4 = ((f32[16,1,1536]{2,1,0:T(1,128)}), f32[16,1,1536]{2,1,0:T(1,128)S(1)}, u32[]{:S(2)}, u32[]{:S(2)}) async-start(f32[16,1,1536]{2,1,0:T(1,128)} %all_to_all.37), calls=%async_computation.4 | async-start | bytes 196608 | tf_op jit(solution)/shard_map/all_to_all | solution.py:101
  130.3 6.8 %all-to-all-done.4 = f32[16,1,1536]{2,1,0:T(1,128)S(1)} async-done(((f32[16,1,1536]{2,1,0:T(1,128)}), f32[16,1,1536]{2,1,0:T(1,128)S(1)}, u32[]{:S(2)}, u32[]{:S(2)}) %all-to-all-start.4) | async-done | bytes 98336 | tf_op jit(solution)/shard_map/all_to_all | solution.py:101
  137.1 3.6 %all-to-all-start.2 = ((bf16[16,2,1,64,128]{4,3,1,2,0:T(8,128)(2,1)}), bf16[16,2,1,64,128]{4,3,1,2,0:T(8,128)(2,1)S(1)}, u32[]{:S(2)}, u32[]{:S(2)}) async-start(bf16[16,2,1,64,128]{4,3,1,2,0:T(8,128)(2,1)} %constant_dynamic-update-slice_fusion.19), calls=%async_computation.2 | async-start | bytes 1048576 | tf_op jit(solution)/shard_map/all_to_all | solution.py:59
  142.6 1.4 convolution_bitcast_fusion.2
  144.1 11.0 %all-to-all-done.2 = bf16[16,2,1,64,128]{4,3,1,2,0:T(8,128)(2,1)S(1)} async-done(((bf16[16,2,1,64,128]{4,3,1,2,0:T(8,128)(2,1)}), bf16[16,2,1,64,128]{4,3,1,2,0:T(8,128)(2,1)S(1)}, u32[]{:S(2)}, u32[]{:S(2)}) %all-to-all-start.2) | async-done | bytes 524320 | tf_op jit(solution)/shard_map/all_to_all | solution.py:59
  155.8 4.0 %all-to-all-start.5 = ((f32[16,1,1536]{2,1,0:T(1,128)}), f32[16,1,1536]{2,1,0:T(1,128)S(1)}, u32[]{:S(2)}, u32[]{:S(2)}) async-start(f32[16,1,1536]{2,1,0:T(1,128)} %broadcast_in_dim.14), calls=%async_computation.5 | async-start | bytes 196608 | tf_op jit(solution)/shard_map/all_to_all | solution.py:104
  162.1 5.2 %all-to-all-done.5 = f32[16,1,1536]{2,1,0:T(1,128)S(1)} async-done(((f32[16,1,1536]{2,1,0:T(1,128)}), f32[16,1,1536]{2,1,0:T(1,128)S(1)}, u32[]{:S(2)}, u32[]{:S(2)}) %all-to-all-start.5) | async-done | bytes 98336 | tf_op jit(solution)/shard_map/all_to_all | solution.py:104
  167.3 3.6 %all-to-all-start.3 = ((bf16[32,1,64,128]{3,2,1,0:T(8,128)(2,1)}), bf16[32,1,64,128]{3,2,1,0:T(8,128)(2,1)S(1)}, u32[]{:S(2)}, u32[]{:S(2)}) async-start(bf16[32,1,64,128]{3,2,1,0:T(8,128)(2,1)} %copy.141), calls=%async_computation.3 | async-start | bytes 1048576 | tf_op jit(solution)/shard_map/all_to_all | solution.py:66
  170.8 2.9 %pad_convert_fusion = f32[4,18,64,130]{3,2,1,0:T(8,128)} fusion(bf16[4,16,64,128]{3,2,1,0:T(8,128)(2,1)S(1)} %pad_maximum_fusion), kind=kLoop, calls=%fused_computation.12 | loop fusion | flops 599040 | bytes 3444736 | tf_op jit(solution)/shard_map/convert_element_type | solution.py:70
  173.8 1.4 convolution_bitcast_fusion.3
  175.2 1.5 convolution_bitcast_fusion.4
  176.7 1.4 convolution_bitcast_fusion
  179.1 6.2 %all-to-all-done.3 = bf16[32,1,64,128]{3,2,1,0:T(8,128)(2,1)S(1)} async-done(((bf16[32,1,64,128]{3,2,1,0:T(8,128)(2,1)}), bf16[32,1,64,128]{3,2,1,0:T(8,128)(2,1)S(1)}, u32[]{:S(2)}, u32[]{:S(2)}) %all-to-all-start.3) | async-done | bytes 524320 | tf_op jit(solution)/shard_map/all_to_all | solution.py:66
  185.3 7.5 %fusion.15 = f32[2,16,64,128]{3,2,1,0:T(8,128)S(1)} fusion(f32[2,16,128,64]{2,3,1,0:T(8,128)} %fusion.73, f32[4,18,64,130]{3,2,1,0:T(8,128)} %pad_convert_fusion, bf16[64,64]{1,0:T(8,128)(2,1)S(1)} %copy-done.14, bf16[16,2,1,64,128]{4,3,1,0,2:T(8,128)(2,1)S(1)} %bitcast.456), kind=kOutput, calls=%fused_computation.40 | convolution fusion | flops 36438016 | bytes 9969664 | tf_op jit(solution)/shard_map/oc,xyoz->xycz/dot_general | solution.py:149
  192.8 3.2 %fusion.16 = bf16[2,16,64,128]{3,2,1,0:T(8,128)(2,1)} fusion(f32[2,16,64,128]{3,2,1,0:T(8,128)S(1)} %copy-done.2, f32[2,16,64,128]{3,2,1,0:T(8,128)S(1)} %convolution_bitcast_fusion.1, f32[2,16,64,128]{3,2,1,0:T(8,128)} %convolution_bitcast_fusion.2, f32[2,16,64,128]{3,2,1,0:T(8,128)} %convolution_bitcast_fusion.3, ...), kind=kOutput, calls=%fused_computation.43 | convolution fusion | flops 35389440 | bytes 7880716 | tf_op jit(solution)/shard_map/oc,xyoz->xycz/dot_general | solution.py:156
  (100 shorter events, 45.7 us)
Async XLA Ops:
  0.6 78.5 %copy-start = (bf16[16,64,64]{2,1,0:T(8,128)(2,1)S(1)}, bf16[16,64,64]{2,1,0:T(8,128)(2,1)}, u32[]{:S(2)}) copy-start(bf16[16,64,64]{2,1,0:T(8,128)(2,1)} %param.18) | copy-start | bytes 393220
  0.6 36.3 %copy-start.1 = (bf16[2,16,64,128]{3,2,1,0:T(8,128)(2,1)S(1)}, bf16[2,16,64,128]{3,2,1,0:T(8,128)(2,1)}, u32[]{:S(2)}) copy-start(bf16[2,16,64,128]{3,2,1,0:T(8,128)(2,1)} %param.10) | copy-start | bytes 1572868
  0.7 36.3 %copy-start.12 = (s32[64]{0:T(128)S(1)}, s32[64]{0:T(128)}, u32[]{:S(2)}) copy-start(s32[64]{0:T(128)} %param.13) | copy-start | bytes 772
  0.7 36.3 %copy-start.6 = (bf16[64,64]{1,0:T(8,128)(2,1)S(1)}, bf16[64,64]{1,0:T(8,128)(2,1)}, u32[]{:S(2)}) copy-start(bf16[64,64]{1,0:T(8,128)(2,1)} %param.15) | copy-start | bytes 24580
  0.7 37.6 %copy-start.8 = (s32[2,16,128]{2,1,0:T(8,128)S(1)}, s32[2,16,128]{2,1,0:T(8,128)}, u32[]{:S(2)}) copy-start(s32[2,16,128]{2,1,0:T(8,128)} %param.12) | copy-start | bytes 49156
  0.7 38.1 %copy-start.7 = (s32[6,3]{0,1:T(4,128)S(1)}, s32[6,3]{0,1:T(4,128)}, u32[]{:S(2)}) copy-start(s32[6,3]{0,1:T(4,128)} %param.14) | copy-start | bytes 220
  1.8 72.2 %collective-permute-start = (bf16[1,16,64,128]{3,2,1,0:T(8,128)(2,1)S(1)}, bf16[1,16,64,128]{3,2,1,0:T(8,128)(2,1)S(1)}, u32[]{:S(2)}, u32[]{:S(2)}) collective-permute-start(bf16[1,16,64,128]{3,2,1,0:T(8,128)(2,1)S(1)} %get-tuple-element.5), channel_id=1, source_target_pairs={{0,1},{1,2},{2,3},{3,4},{4,5},{5,6},{6,7},{7,8},{8,9},{9,10},{10,1... | collective-permute-start | bytes 786440 | tf_op jit(solution)/shard_map/ppermute | solution.py:19
  4.2 70.0 %collective-permute-start.1 = (bf16[1,16,64,128]{3,2,1,0:T(8,128)(2,1)S(1)}, bf16[1,16,64,128]{3,2,1,0:T(8,128)(2,1)S(1)}, u32[]{:S(2)}, u32[]{:S(2)}) collective-permute-start(bf16[1,16,64,128]{3,2,1,0:T(8,128)(2,1)S(1)} %get-tuple-element.4), channel_id=1, source_target_pairs={{1,0},{2,1},{3,2},{4,3},{5,4},{6,5},{7,6},{8,7},{9,8},{10,9},{11,1... | collective-permute-start | bytes 786440 | tf_op jit(solution)/shard_map/ppermute | solution.py:21
  27.5 46.7 %copy-start.5 = (bf16[6,64,64]{2,1,0:T(8,128)(2,1)S(1)}, bf16[6,64,64]{2,1,0:T(8,128)(2,1)}, u32[]{:S(2)}) copy-start(bf16[6,64,64]{2,1,0:T(8,128)(2,1)} %param.16) | copy-start | bytes 147460
  27.5 50.0 %all-to-all-start = ((bf16[16,2,1,64,128]{4,3,1,2,0:T(8,128)(2,1)}), bf16[16,2,1,64,128]{4,3,1,2,0:T(8,128)(2,1)S(1)}, u32[]{:S(2)}, u32[]{:S(2)}) async-start(bf16[16,2,1,64,128]{4,3,1,2,0:T(8,128)(2,1)} %constant_dynamic-update-slice_fusion.3), calls=%async_computation | async-start | bytes 1048576 | tf_op jit(solution)/shard_map/all_to_all | solution.py:59
  81.5 20.5 %all-to-all-start.1 = ((bf16[32,1,64,128]{3,2,1,0:T(8,128)(2,1)}), bf16[32,1,64,128]{3,2,1,0:T(8,128)(2,1)S(1)}, u32[]{:S(2)}, u32[]{:S(2)}) async-start(bf16[32,1,64,128]{3,2,1,0:T(8,128)(2,1)} %copy.116), calls=%async_computation.1 | async-start | bytes 1048576 | tf_op jit(solution)/shard_map/all_to_all | solution.py:66
  88.3 2.9 %copy-start.4 = (f32[2,16,128,64]{2,3,1,0:T(8,128)S(1)}, f32[2,16,128,64]{2,3,1,0:T(8,128)}, u32[]{:S(2)}) copy-start(f32[2,16,128,64]{2,3,1,0:T(8,128)} %fusion.75) | copy-start | bytes 3145732
  88.3 2.9 %copy-start.13 = (bf16[64,64]{1,0:T(8,128)(2,1)S(1)}, bf16[64,64]{1,0:T(8,128)(2,1)}, u32[]{:S(2)}) copy-start(bf16[64,64]{1,0:T(8,128)(2,1)} %param.17) | copy-start | bytes 24580
  89.7 13.0 %copy-start.11 = (f32[64]{0:T(128)S(1)}, f32[64]{0:T(128)}, u32[]{:S(2)}) copy-start(f32[64]{0:T(128)} %param.19) | copy-start | bytes 772
  102.0 0.8 copy-start.3
  107.6 11.9 %collective-permute-start.2 = (bf16[1,16,64,128]{3,2,1,0:T(8,128)(2,1)S(1)}, bf16[1,16,64,128]{3,2,1,0:T(8,128)(2,1)S(1)}, u32[]{:S(2)}, u32[]{:S(2)}) collective-permute-start(bf16[1,16,64,128]{3,2,1,0:T(8,128)(2,1)S(1)} %get-tuple-element.2), channel_id=1, source_target_pairs={{0,1},{1,2},{2,3},{3,4},{4,5},{5,6},{6,7},{7,8},{8,9},{9,10},{10,1... | collective-permute-start | bytes 786440 | tf_op jit(solution)/shard_map/ppermute | solution.py:19
  109.6 10.0 %collective-permute-start.3 = (bf16[1,16,64,128]{3,2,1,0:T(8,128)(2,1)S(1)}, bf16[1,16,64,128]{3,2,1,0:T(8,128)(2,1)S(1)}, u32[]{:S(2)}, u32[]{:S(2)}) collective-permute-start(bf16[1,16,64,128]{3,2,1,0:T(8,128)(2,1)S(1)} %get-tuple-element.3), channel_id=1, source_target_pairs={{1,0},{2,1},{3,2},{4,3},{5,4},{6,5},{7,6},{8,7},{9,8},{10,9},{11,1... | collective-permute-start | bytes 786440 | tf_op jit(solution)/shard_map/ppermute | solution.py:21
  122.8 14.3 %all-to-all-start.4 = ((f32[16,1,1536]{2,1,0:T(1,128)}), f32[16,1,1536]{2,1,0:T(1,128)S(1)}, u32[]{:S(2)}, u32[]{:S(2)}) async-start(f32[16,1,1536]{2,1,0:T(1,128)} %all_to_all.37), calls=%async_computation.4 | async-start | bytes 196608 | tf_op jit(solution)/shard_map/all_to_all | solution.py:101
  137.1 18.0 %all-to-all-start.2 = ((bf16[16,2,1,64,128]{4,3,1,2,0:T(8,128)(2,1)}), bf16[16,2,1,64,128]{4,3,1,2,0:T(8,128)(2,1)S(1)}, u32[]{:S(2)}, u32[]{:S(2)}) async-start(bf16[16,2,1,64,128]{4,3,1,2,0:T(8,128)(2,1)} %constant_dynamic-update-slice_fusion.19), calls=%async_computation.2 | async-start | bytes 1048576 | tf_op jit(solution)/shard_map/all_to_all | solution.py:59
  142.2 17.7 %copy-start.9 = (f32[16]{0:T(128)S(1)}, f32[16]{0:T(128)}, u32[]{:S(2)}) copy-start(f32[16]{0:T(128)} %get-tuple-element.27) | copy-start | bytes 196
  142.2 17.7 %copy-start.10 = (f32[32]{0:T(128)S(1)}, f32[32]{0:T(128)}, u32[]{:S(2)}) copy-start(f32[32]{0:T(128)} %multiply_add_fusion) | copy-start | bytes 388
  155.8 11.4 %all-to-all-start.5 = ((f32[16,1,1536]{2,1,0:T(1,128)}), f32[16,1,1536]{2,1,0:T(1,128)S(1)}, u32[]{:S(2)}, u32[]{:S(2)}) async-start(f32[16,1,1536]{2,1,0:T(1,128)} %broadcast_in_dim.14), calls=%async_computation.5 | async-start | bytes 196608 | tf_op jit(solution)/shard_map/all_to_all | solution.py:104
  167.3 18.0 %all-to-all-start.3 = ((bf16[32,1,64,128]{3,2,1,0:T(8,128)(2,1)}), bf16[32,1,64,128]{3,2,1,0:T(8,128)(2,1)S(1)}, u32[]{:S(2)}, u32[]{:S(2)}) async-start(bf16[32,1,64,128]{3,2,1,0:T(8,128)(2,1)} %copy.141), calls=%async_computation.3 | async-start | bytes 1048576 | tf_op jit(solution)/shard_map/all_to_all | solution.py:66
  175.2 10.1 %copy-start.14 = (bf16[64,64]{1,0:T(8,128)(2,1)S(1)}, bf16[64,64]{1,0:T(8,128)(2,1)}, u32[]{:S(2)}) copy-start(bf16[64,64]{1,0:T(8,128)(2,1)} %param.17) | copy-start | bytes 24580
  185.3 7.5 %copy-start.2 = (f32[2,16,64,128]{3,2,1,0:T(8,128)S(1)}, f32[2,16,64,128]{3,2,1,0:T(8,128)}, u32[]{:S(2)}) copy-start(f32[2,16,64,128]{3,2,1,0:T(8,128)} %convolution_bitcast_fusion) | copy-start | bytes 3145732
